TPU v7x, 256 devices: a whole 4x4x8 slice. The times are simulated.
256 devices in a mesh: dp: 32 (over x, z), fsdp: 8 (over y, core).
Axes of the slice: x: 4, y: 4, z: 8, core: 2. Of those that a mesh axis runs over, the one named last changes fastest.
Arguments:
- hidden: bfloat16 [8192, 28672], P('dp', 'fsdp'), may hold values from -6 to 6
- cotangent: bfloat16 [8192, 8192], P('dp', 'fsdp'), may hold values from -6 to 6
- region_ids: int32 [8192], P('dp'), may hold values from 0 to 255, as said below
- adapter_a: bfloat16 [256, 64, 28672], P('dp', None, 'fsdp'), may hold values from -0.03125 to 0.03125
- adapter_b: bfloat16 [256, 64, 8192], P('dp', None, 'fsdp'), may hold values from -0.75 to 0.75
Outputs:
- grad_a: bfloat16 [256, 64, 28672], P('dp', None, 'fsdp')
- grad_b: bfloat16 [256, 64, 8192], P('dp', None, 'fsdp')
- grad_hidden: bfloat16 [8192, 28672], P('dp', 'fsdp')
Inputs may be any that keep to these rules, and one draw needn't show every extreme that they name: `region_ids`: region r belongs to owner r // 8. In each aligned block of 256 tokens (the tokens of one index of dp) the ids never fall, and at most 24 tokens name regions of one owner; in every block 4 owners, the same ones in every block, reach that bound.
All inputs are finite; a program needn't handle non-finite values.
Results may differ from a plain program's by a relative error of at most 0.0049.
Values may be sent and summed in bfloat16 or wider, within the bound.
A program may use at most 128 MiB of HBM per device.

v0:
```python
import jax
import jax.numpy as jnp
from jax import lax
from jax.sharding import PartitionSpec as P


def contract_rows(left, right):
    return lax.dot_general(
        left, right, (((0,), (0,)), ((), ())), preferred_element_type=jnp.float32
    )


def contract_cols(left, right):
    return lax.dot_general(
        left, right, (((1,), (1,)), ((), ())), preferred_element_type=jnp.float32
    )


def shards(hidden, cotangent, region_ids, adapter_a, adapter_b):
    owner_count = lax.axis_size("dp")
    token_count = hidden.shape[0]
    local_count = adapter_a.shape[0]
    rank_width = adapter_a.shape[1]
    hidden_width = hidden.shape[1]
    model_width = cotangent.shape[1]
    capacity = 3 * token_count // owner_count
    owner_of = region_ids // local_count
    owner_ids = jnp.arange(owner_count, dtype=jnp.int32)
    counts = jnp.sum((owner_of[:, None] == owner_ids[None, :]).astype(jnp.int32), axis=0)
    starts = jnp.cumsum(counts) - counts
    slot_index = jnp.arange(capacity, dtype=jnp.int32)
    usable = slot_index[None, :] < counts[:, None]
    row_index = jnp.where(usable, starts[:, None] + slot_index[None, :], token_count)
    id_width = 128
    table = jnp.concatenate(
        [
            hidden,
            cotangent,
            jnp.broadcast_to(
                (region_ids % local_count).astype(jnp.bfloat16)[:, None], (token_count, id_width)
            ),
        ],
        axis=-1,
    )
    flat_a = adapter_a.reshape(local_count * rank_width, hidden_width)
    flat_b = adapter_b.reshape(local_count * rank_width, model_width)
    local_ids = jnp.arange(local_count).astype(jnp.bfloat16)
    pieces = 2
    piece = capacity // pieces
    grad_a = None
    grad_b = None
    arrived = []
    for k in range(pieces):
        send = table.at[row_index[:, k * piece : (k + 1) * piece]].get(
            mode="fill", fill_value=local_count
        )
        recv = lax.all_to_all(send, "dp", split_axis=0, concat_axis=0, tiled=True)
        if k > 0:
            recv, full = lax.optimization_barrier((recv, full))
        rows = owner_count * piece
        recv = recv.reshape(rows, hidden_width + model_width + id_width)
        got_hidden = recv[:, :hidden_width]
        got_cotangent = recv[:, hidden_width : hidden_width + model_width]
        got_local = recv[:, hidden_width + model_width]
        onehot = (got_local[:, None] == local_ids[None, :]).astype(jnp.float32)
        part_down = contract_cols(got_hidden, flat_a).reshape(rows, local_count, rank_width)
        part_back = contract_cols(got_cotangent, flat_b).reshape(rows, local_count, rank_width)
        pick_down = jnp.sum(part_down * onehot[:, :, None], axis=1)
        pick_back = jnp.sum(part_back * onehot[:, :, None], axis=1)
        full = lax.psum(jnp.concatenate([pick_down, pick_back], axis=1), "fsdp")
        full_down = full[:, :rank_width].astype(jnp.bfloat16)
        full_back = full[:, rank_width:].astype(jnp.bfloat16)
        mask = onehot.astype(jnp.bfloat16)[:, :, None]
        down_rows = (mask * full_down[:, None, :]).reshape(rows, local_count * rank_width)
        back_rows = (mask * full_back[:, None, :]).reshape(rows, local_count * rank_width)
        returned = jnp.dot(back_rows, flat_a, preferred_element_type=jnp.float32).astype(
            jnp.bfloat16
        )
        returned = returned.reshape(owner_count, piece, hidden_width)
        arrived.append(lax.all_to_all(returned, "dp", split_axis=0, concat_axis=0, tiled=True))
        part_b = contract_rows(down_rows, got_cotangent)
        part_a = contract_rows(back_rows, got_hidden)
        grad_b = part_b if grad_b is None else grad_b + part_b
        grad_a = part_a if grad_a is None else grad_a + part_a
    grad_b = grad_b.reshape(local_count, rank_width, model_width).astype(jnp.bfloat16)
    grad_a = grad_a.reshape(local_count, rank_width, hidden_width).astype(jnp.bfloat16)
    arrived = jnp.concatenate(arrived, axis=1)
    before = jnp.sum((owner_of[None, :] < owner_of[:, None]).astype(jnp.int32), axis=1)
    position = jnp.arange(token_count, dtype=jnp.int32) - before
    grad_hidden = arrived.reshape(owner_count * capacity, hidden_width)[
        owner_of * capacity + position
    ]
    return (grad_a, grad_b, grad_hidden)


def solution(mesh):
    return jax.shard_map(
        shards,
        mesh=mesh,
        in_specs=(
            P("dp", "fsdp"),
            P("dp", "fsdp"),
            P("dp"),
            P("dp", None, "fsdp"),
            P("dp", None, "fsdp"),
        ),
        out_specs=(P("dp", None, "fsdp"), P("dp", None, "fsdp"), P("dp", "fsdp")),
        check_vma=False,
    )
```

profile of v0, /device:TPU:24, one launch (start us, length us, event | category | flops | bytes accessed | tf_op | source)
XLA Modules:
  0.0 509.1 jit_solution(9303705913638020247)
XLA Ops:
  4.1 4.6 gather_fusion
  8.7 6.8 %reshape.229 = bf16[32,12,4736]{2,1,0:T(8,128)(2,1)} reshape(bf16[384,4736]{1,0:T(8,128)(2,1)} %gather_fusion) | data formatting | bytes 7274496 | tf_op jit(solution)/shard_map/gather | solution.py:54
  15.5 5.2 %broadcast_select_fusion.1 = bf16[32,12,4736]{2,1,0:T(8,128)(2,1)} fusion(bf16[32,12,4736]{2,1,0:T(8,128)(2,1)} %reshape.229, pred[32,12]{1,0:T(8,128)(4,1)S(1)} %get-tuple-element.10), kind=kLoop, calls=%fused_computation.10 | loop fusion | flops 1818624 | bytes 7274880 | tf_op jit(solution)/shard_map/select_n | solution.py:54
  20.6 11.4 %all-to-all-start = ((bf16[32,12,4736]{2,1,0:T(8,128)(2,1)}), bf16[32,12,4736]{2,1,0:T(8,128)(2,1)}, u32[]{:S(2)}, u32[]{:S(2)}) async-start(bf16[32,12,4736]{2,1,0:T(8,128)(2,1)} %broadcast_select_fusion.1), calls=%async_computation | async-start | bytes 9699328 | tf_op jit(solution)/shard_map/all_to_all | solution.py:57
  36.8 6.8 %reshape.237 = bf16[32,12,4736]{2,1,0:T(8,128)(2,1)} reshape(bf16[384,4736]{1,0:T(8,128)(2,1)} %gather_fusion.1) | data formatting | bytes 7274496 | tf_op jit(solution)/shard_map/gather | solution.py:54
  43.5 5.2 %broadcast_select_fusion = bf16[32,12,4736]{2,1,0:T(8,128)(2,1)} fusion(bf16[32,12,4736]{2,1,0:T(8,128)(2,1)} %reshape.237, pred[32,12]{1,0:T(8,128)(4,1)S(1)} %get-tuple-element.9), kind=kLoop, calls=%fused_computation.9 | loop fusion | flops 1818624 | bytes 7274880 | tf_op jit(solution)/shard_map/select_n | solution.py:54
  48.8 92.7 %all-to-all-done = bf16[32,12,4736]{2,1,0:T(8,128)(2,1)} async-done(((bf16[32,12,4736]{2,1,0:T(8,128)(2,1)}), bf16[32,12,4736]{2,1,0:T(8,128)(2,1)}, u32[]{:S(2)}, u32[]{:S(2)}) %all-to-all-start) | async-done | bytes 3637280 | tf_op jit(solution)/shard_map/all_to_all | solution.py:57
  141.5 7.7 %all-to-all-start.1 = ((bf16[32,12,4736]{2,1,0:T(8,128)(2,1)}), bf16[32,12,4736]{2,1,0:T(8,128)(2,1)}, u32[]{:S(2)}, u32[]{:S(2)}) async-start(bf16[32,12,4736]{2,1,0:T(8,128)(2,1)} %broadcast_select_fusion), calls=%async_computation.1 | async-start | bytes 9699328 | tf_op jit(solution)/shard_map/all_to_all | solution.py:57
  149.2 6.9 %reshape.223 = bf16[384,4736]{1,0:T(8,128)(2,1)} reshape(bf16[32,12,4736]{2,1,0:T(8,128)(2,1)} %all-to-all-done) | data formatting | bytes 7274496 | tf_op jit(solution)/shard_map/reshape | solution.py:61
  163.1 25.8 %all-reduce.2 = bf16[384,128]{0,1:T(8,128)(2,1)S(1)} all-reduce(f32[384,128]{0,1:T(8,128)S(1)} %pad_maximum_fusion.2), channel_id=1, replica_groups=mesh['dp'=32,'fsdp'=8] {'fsdp'}, use_global_device_ids=true, to_apply=%region_4.5 | all-reduce | flops 49152 | bytes 294912 | tf_op jit(solution)/shard_map/psum | solution.py:70
  188.9 69.3 %all-to-all-done.1 = bf16[32,12,4736]{2,1,0:T(8,128)(2,1)} async-done(((bf16[32,12,4736]{2,1,0:T(8,128)(2,1)}), bf16[32,12,4736]{2,1,0:T(8,128)(2,1)}, u32[]{:S(2)}, u32[]{:S(2)}) %all-to-all-start.1) | async-done | bytes 3637280 | tf_op jit(solution)/shard_map/all_to_all | solution.py:57
  258.2 6.9 %reshape.224 = bf16[384,4736]{1,0:T(8,128)(2,1)} reshape(bf16[32,12,4736]{2,1,0:T(8,128)(2,1)} %all-to-all-done.1) | data formatting | bytes 7274496 | tf_op jit(solution)/shard_map/reshape | solution.py:61
  266.2 5.0 fusion.19
  273.0 22.5 %all-reduce.3 = bf16[384,128]{0,1:T(8,128)(2,1)S(1)} all-reduce(f32[384,128]{0,1:T(8,128)S(1)} %pad_maximum_fusion.3), channel_id=1, replica_groups=mesh['dp'=32,'fsdp'=8] {'fsdp'}, use_global_device_ids=true, to_apply=%region_7.8 | all-reduce | flops 49152 | bytes 294912 | tf_op jit(solution)/shard_map/psum | solution.py:70
  295.5 5.2 %fusion.1 = bf16[384,3584]{1,0:T(8,128)(2,1)} fusion(bf16[8,64,3584]{2,1,0:T(8,128)(2,1)} %param.8, bf16[384,64]{0,1:T(8,128)(2,1)S(1)} %get-tuple-element.6, bf16[384,8]{0,1:T(8,128)(2,1)S(1)} %get-tuple-element.17), kind=kOutput, calls=%fused_computation.7 | convolution fusion | flops 1410859008 | bytes 6477824 | tf_op jit(solution)/shard_map/dot_general | solution.py:76
  300.8 5.3 %reshape.226 = bf16[32,12,3584]{2,1,0:T(8,128)(2,1)} reshape(bf16[384,3584]{1,0:T(8,128)(2,1)} %fusion.1) | data formatting | bytes 5505024 | tf_op jit(solution)/shard_map/reshape | solution.py:79
  306.0 10.0 %all-to-all-start.3 = ((bf16[32,12,3584]{2,1,0:T(8,128)(2,1)}), bf16[32,12,3584]{2,1,0:T(8,128)(2,1)}, u32[]{:S(2)}, u32[]{:S(2)}) async-start(bf16[32,12,3584]{2,1,0:T(8,128)(2,1)} %reshape.226), calls=%async_computation.3 | async-start | bytes 7340032 | tf_op jit(solution)/shard_map/all_to_all | solution.py:80
  316.0 5.2 %fusion = bf16[384,3584]{1,0:T(8,128)(2,1)} fusion(bf16[8,64,3584]{2,1,0:T(8,128)(2,1)} %param.8, bf16[384,64]{0,1:T(8,128)(2,1)S(1)} %get-tuple-element.8, bf16[384,8]{0,1:T(8,128)(2,1)S(1)} %get-tuple-element.19), kind=kOutput, calls=%fused_computation.6 | convolution fusion | flops 1410859008 | bytes 6477824 | tf_op jit(solution)/shard_map/dot_general | solution.py:76
  321.2 5.3 %reshape.225 = bf16[32,12,3584]{2,1,0:T(8,128)(2,1)} reshape(bf16[384,3584]{1,0:T(8,128)(2,1)} %fusion) | data formatting | bytes 5505024 | tf_op jit(solution)/shard_map/reshape | solution.py:79
  326.5 74.0 %all-to-all-done.3 = bf16[32,12,3584]{2,1,0:T(8,128)(2,1)} async-done(((bf16[32,12,3584]{2,1,0:T(8,128)(2,1)}), bf16[32,12,3584]{2,1,0:T(8,128)(2,1)}, u32[]{:S(2)}, u32[]{:S(2)}) %all-to-all-start.3) | async-done | bytes 2752544 | tf_op jit(solution)/shard_map/all_to_all | solution.py:80
  400.5 7.4 %all-to-all-start.2 = ((bf16[32,12,3584]{2,1,0:T(8,128)(2,1)}), bf16[32,12,3584]{2,1,0:T(8,128)(2,1)}, u32[]{:S(2)}, u32[]{:S(2)}) async-start(bf16[32,12,3584]{2,1,0:T(8,128)(2,1)} %reshape.225), calls=%async_computation.2 | async-start | bytes 7340032 | tf_op jit(solution)/shard_map/all_to_all | solution.py:80
  418.1 75.9 %all-to-all-done.2 = bf16[32,12,3584]{2,1,0:T(8,128)(2,1)} async-done(((bf16[32,12,3584]{2,1,0:T(8,128)(2,1)}), bf16[32,12,3584]{2,1,0:T(8,128)(2,1)}, u32[]{:S(2)}, u32[]{:S(2)}) %all-to-all-start.2) | async-done | bytes 2752544 | tf_op jit(solution)/shard_map/all_to_all | solution.py:80
  493.9 7.1 %pad_maximum_fusion = bf16[32,24,3584]{2,1,0:T(8,128)(2,1)} fusion(bf16[32,12,3584]{2,1,0:T(8,128)(2,1)} %all-to-all-done.3, bf16[32,12,3584]{2,1,0:T(8,128)(2,1)} %all-to-all-done.2), kind=kLoop, calls=%fused_computation.8 | loop fusion | flops 11010048 | bytes 11010048 | tf_op jit(solution)/shard_map/concatenate | solution.py:87
  501.0 8.0 %gather_fusion.2 = bf16[256,3584]{1,0:T(8,128)(2,1)} fusion(bf16[768,3584]{1,0:T(8,128)(2,1)} %bitcast.46, s32[1024]{0:T(1024)S(1)} %pad_clamp_fusion), kind=kCustom, calls=%fused_computation.2 | custom fusion | bytes 3671040 | tf_op jit(solution)/shard_map/gather | solution.py:90
  (45 shorter events, 28.2 us)
Async XLA Ops:
  0.6 156.7 %copy-start = (bf16[8,64,1024]{2,1,0:T(8,128)(2,1)S(1)}, bf16[8,64,1024]{2,1,0:T(8,128)(2,1)}, u32[]{:S(2)}) copy-start(bf16[8,64,1024]{2,1,0:T(8,128)(2,1)} %param.9) | copy-start | bytes 3145732
  20.6 120.8 %all-to-all-start = ((bf16[32,12,4736]{2,1,0:T(8,128)(2,1)}), bf16[32,12,4736]{2,1,0:T(8,128)(2,1)}, u32[]{:S(2)}, u32[]{:S(2)}) async-start(bf16[32,12,4736]{2,1,0:T(8,128)(2,1)} %broadcast_select_fusion.1), calls=%async_computation | async-start | bytes 9699328 | tf_op jit(solution)/shard_map/all_to_all | solution.py:57
  141.5 116.8 %all-to-all-start.1 = ((bf16[32,12,4736]{2,1,0:T(8,128)(2,1)}), bf16[32,12,4736]{2,1,0:T(8,128)(2,1)}, u32[]{:S(2)}, u32[]{:S(2)}) async-start(bf16[32,12,4736]{2,1,0:T(8,128)(2,1)} %broadcast_select_fusion), calls=%async_computation.1 | async-start | bytes 9699328 | tf_op jit(solution)/shard_map/all_to_all | solution.py:57
  156.1 3.1 copy-start.1
  306.0 94.5 %all-to-all-start.3 = ((bf16[32,12,3584]{2,1,0:T(8,128)(2,1)}), bf16[32,12,3584]{2,1,0:T(8,128)(2,1)}, u32[]{:S(2)}, u32[]{:S(2)}) async-start(bf16[32,12,3584]{2,1,0:T(8,128)(2,1)} %reshape.226), calls=%async_computation.3 | async-start | bytes 7340032 | tf_op jit(solution)/shard_map/all_to_all | solution.py:80
  400.5 93.4 %all-to-all-start.2 = ((bf16[32,12,3584]{2,1,0:T(8,128)(2,1)}), bf16[32,12,3584]{2,1,0:T(8,128)(2,1)}, u32[]{:S(2)}, u32[]{:S(2)}) async-start(bf16[32,12,3584]{2,1,0:T(8,128)(2,1)} %reshape.225), calls=%async_computation.2 | async-start | bytes 7340032 | tf_op jit(solution)/shard_map/all_to_all | solution.py:80
  407.9 2.5 copy-start.3
  408.3 3.8 copy-start.2
where the time goes:
time: 511 us; the launch traced here: 509 us
  waiting for transfers between devices  312 us (61%)
  local copies, waits for them, and re-layouts  57.6 us (11%)
  blocking collectives  48.2 us (9%)
  starting transfers between devices  36.5 us (7%)
  matrix products  32.7 us (6%)
  other arithmetic  21.2 us (4%)
    all_to_all x2, waiting for transfers between devices, shards(): recv = lax.all_to_all(send, 'dp', split_axis=0, concat_axis=0, tiled=True)  162 us
    all_to_all x2, waiting for transfers between devices, shards(): lax.all_to_all(returned, 'dp', split_axis=0, concat_axis=0, tiled=True)  150 us
    psum x2, blocking collectives, shards(): full = lax.psum(jnp.concatenate([pick_down, pick_back], axis=1), 'fsdp')  48.2 us
    gather x4, local copies, waits for them, and re-layouts, shards(): table.at[row_index[:, k * piece:(k + 1) * piece]]  22.7 us
    all_to_all x2, starting transfers between devices, shards(): recv = lax.all_to_all(send, 'dp', split_axis=0, concat_axis=0, tiled=True)  19.1 us
    all_to_all x2, starting transfers between devices, shards(): lax.all_to_all(returned, 'dp', split_axis=0, concat_axis=0, tiled=True)  17.4 us
    reshape x2, local copies, waits for them, and re-layouts, shards(): recv = recv.reshape(rows, hidden_width + model_width + id_width)  13.7 us
    dot_general x4, matrix products, contract_cols(): lax.dot_general(left, right, (((1,), (1,)), ((), ())), preferred_element_...  12.6 us
  transfers between devices with their start and end apart: 4, of which 4 were waited for; matrix products, arithmetic and copies ran while one was open for 10% of the time, Pallas kernels for 0%

commit v1 on v0

--- a/solution.py
+++ b/solution.py
@@ -67,7 +67,9 @@
         part_back = contract_cols(got_cotangent, flat_b).reshape(rows, local_count, rank_width)
         pick_down = jnp.sum(part_down * onehot[:, :, None], axis=1)
         pick_back = jnp.sum(part_back * onehot[:, :, None], axis=1)
-        full = lax.psum(jnp.concatenate([pick_down, pick_back], axis=1), "fsdp")
+        block = jnp.concatenate([pick_down, pick_back], axis=1)
+        parts = lax.all_gather(block, "fsdp", axis=0, tiled=False)
+        full = parts.sum(axis=0)
         full_down = full[:, :rank_width].astype(jnp.bfloat16)
         full_back = full[:, rank_width:].astype(jnp.bfloat16)
         mask = onehot.astype(jnp.bfloat16)[:, :, None]

time: 511 us -> 473 us (0.926)
  blocking collectives: 48.2 us -> 0 us
  between operations: 0.88 us -> 14.3 us
  matrix products: 32.7 us -> 27.5 us
    all_gather x0 -> x2, waiting for transfers between devices: none -> 52.9 us  [shards(): parts = lax.all_gather(block, 'fsdp', axis=0, tiled=False)]
    psum x2 -> x0, blocking collectives: 48.2 us -> none  [shards(): full = lax.psum(jnp.concatenate([pick_down, pick_back], axis=1), 'fsdp')]
    all_to_all x2, waiting for transfers between devices: 150 us -> 109 us  [shards(): lax.all_to_all(returned, 'dp', split_axis=0, concat_axis=0, tiled=True)]
    all_to_all x2, waiting for transfers between devices: 162 us -> 150 us  [shards(): recv = lax.all_to_all(send, 'dp', split_axis=0, concat_axis=0, tiled=True)]
  transfers between devices with their start and end apart: 4 -> 6, of which waited for: 4 -> 6; matrix products, arithmetic and copies ran while one was open for 10% -> 16% of each run, Pallas kernels for 0% -> 0%
where the time goes in v1:
time: 473 us; the launch traced here: 471 us
  waiting for transfers between devices  312 us (66%)
  local copies, waits for them, and re-layouts  61.9 us (13%)
  starting transfers between devices  32.8 us (7%)
  matrix products  27.5 us (6%)
  other arithmetic  23.3 us (5%)
  between operations  14.3 us (3%)
    all_to_all x2, waiting for transfers between devices, shards(): recv = lax.all_to_all(send, 'dp', split_axis=0, concat_axis=0, tiled=True)  150 us
    all_to_all x2, waiting for transfers between devices, shards(): lax.all_to_all(returned, 'dp', split_axis=0, concat_axis=0, tiled=True)  109 us
    all_gather x2, waiting for transfers between devices, shards(): parts = lax.all_gather(block, 'fsdp', axis=0, tiled=False)  52.9 us
    gather x4, local copies, waits for them, and re-layouts, shards(): table.at[row_index[:, k * piece:(k + 1) * piece]]  22.7 us
    all_to_all x2, starting transfers between devices, shards(): recv = lax.all_to_all(send, 'dp', split_axis=0, concat_axis=0, tiled=True)  19.1 us
    reshape x2, local copies, waits for them, and re-layouts, shards(): recv = recv.reshape(rows, hidden_width + model_width + id_width)  13.7 us
    all_to_all x2, starting transfers between devices, shards(): lax.all_to_all(returned, 'dp', split_axis=0, concat_axis=0, tiled=True)  13.4 us
    dot_general x4, matrix products, contract_cols(): lax.dot_general(left, right, (((1,), (1,)), ((), ())), preferred_element_...  11.5 us
  transfers between devices with their start and end apart: 6, of which 6 were waited for; matrix products, arithmetic and copies ran while one was open for 16% of the time, Pallas kernels for 0%

profile of v1, /device:TPU:24, one launch (start us, length us, event | category | flops | bytes accessed | tf_op | source)
XLA Modules:
  0.0 471.4 jit_solution(16651891020978609080)
XLA Ops:
  10.7 4.6 gather_fusion
  15.2 6.8 %reshape.229 = bf16[32,12,4736]{2,1,0:T(8,128)(2,1)} reshape(bf16[384,4736]{1,0:T(8,128)(2,1)} %gather_fusion) | data formatting | bytes 7274496 | tf_op jit(solution)/shard_map/gather | solution.py:54
  22.0 5.2 %broadcast_select_fusion.1 = bf16[32,12,4736]{2,1,0:T(8,128)(2,1)} fusion(bf16[32,12,4736]{2,1,0:T(8,128)(2,1)} %reshape.229, pred[32,12]{1,0:T(8,128)(4,1)S(1)} %get-tuple-element.10), kind=kLoop, calls=%fused_computation.10 | loop fusion | flops 1818624 | bytes 7274880 | tf_op jit(solution)/shard_map/select_n | solution.py:54
  27.2 11.4 %all-to-all-start = ((bf16[32,12,4736]{2,1,0:T(8,128)(2,1)}), bf16[32,12,4736]{2,1,0:T(8,128)(2,1)}, u32[]{:S(2)}, u32[]{:S(2)}) async-start(bf16[32,12,4736]{2,1,0:T(8,128)(2,1)} %broadcast_select_fusion.1), calls=%async_computation | async-start | bytes 9699328 | tf_op jit(solution)/shard_map/all_to_all | solution.py:57
  38.7 4.6 gather_fusion.1
  43.3 6.8 %reshape.237 = bf16[32,12,4736]{2,1,0:T(8,128)(2,1)} reshape(bf16[384,4736]{1,0:T(8,128)(2,1)} %gather_fusion.1) | data formatting | bytes 7274496 | tf_op jit(solution)/shard_map/gather | solution.py:54
  50.1 5.1 %broadcast_select_fusion = bf16[32,12,4736]{2,1,0:T(8,128)(2,1)} fusion(bf16[32,12,4736]{2,1,0:T(8,128)(2,1)} %reshape.237, pred[32,12]{1,0:T(8,128)(4,1)S(1)} %get-tuple-element.9), kind=kLoop, calls=%fused_computation.9 | loop fusion | flops 1818624 | bytes 7274880 | tf_op jit(solution)/shard_map/select_n | solution.py:54
  55.2 92.8 %all-to-all-done = bf16[32,12,4736]{2,1,0:T(8,128)(2,1)} async-done(((bf16[32,12,4736]{2,1,0:T(8,128)(2,1)}), bf16[32,12,4736]{2,1,0:T(8,128)(2,1)}, u32[]{:S(2)}, u32[]{:S(2)}) %all-to-all-start) | async-done | bytes 3637280 | tf_op jit(solution)/shard_map/all_to_all | solution.py:57
  148.0 7.7 %all-to-all-start.1 = ((bf16[32,12,4736]{2,1,0:T(8,128)(2,1)}), bf16[32,12,4736]{2,1,0:T(8,128)(2,1)}, u32[]{:S(2)}, u32[]{:S(2)}) async-start(bf16[32,12,4736]{2,1,0:T(8,128)(2,1)} %broadcast_select_fusion), calls=%async_computation.1 | async-start | bytes 9699328 | tf_op jit(solution)/shard_map/all_to_all | solution.py:57
  155.8 6.9 %reshape.223 = bf16[384,4736]{1,0:T(8,128)(2,1)} reshape(bf16[32,12,4736]{2,1,0:T(8,128)(2,1)} %all-to-all-done) | data formatting | bytes 7274496 | tf_op jit(solution)/shard_map/reshape | solution.py:61
  170.3 26.5 %all-gather.5.cloned.1.call-done = f32[3072,128]{0,1:T(8,128)} async-done(((f32[384,128]{0,1:T(8,128)}), f32[3072,128]{0,1:T(8,128)}) %all-gather.5.cloned.1.call-update) | async-done | bytes 1572880 | tf_op jit(solution)/shard_map/all_gather | solution.py:71
  202.5 5.3 %reshape.225 = bf16[32,12,3584]{2,1,0:T(8,128)(2,1)} reshape(bf16[384,3584]{1,0:T(8,128)(2,1)} %fusion) | data formatting | bytes 5505024 | tf_op jit(solution)/shard_map/reshape | solution.py:81
  207.7 57.0 %all-to-all-done.1 = bf16[32,12,4736]{2,1,0:T(8,128)(2,1)} async-done(((bf16[32,12,4736]{2,1,0:T(8,128)(2,1)}), bf16[32,12,4736]{2,1,0:T(8,128)(2,1)}, u32[]{:S(2)}, u32[]{:S(2)}) %all-to-all-start.1) | async-done | bytes 3637280 | tf_op jit(solution)/shard_map/all_to_all | solution.py:57
  264.8 7.9 %all-to-all-start.2 = ((bf16[32,12,3584]{2,1,0:T(8,128)(2,1)}), bf16[32,12,3584]{2,1,0:T(8,128)(2,1)}, u32[]{:S(2)}, u32[]{:S(2)}) async-start(bf16[32,12,3584]{2,1,0:T(8,128)(2,1)} %reshape.225), calls=%async_computation.2 | async-start | bytes 7340032 | tf_op jit(solution)/shard_map/all_to_all | solution.py:82
  272.9 6.9 %reshape.224 = bf16[384,4736]{1,0:T(8,128)(2,1)} reshape(bf16[32,12,4736]{2,1,0:T(8,128)(2,1)} %all-to-all-done.1) | data formatting | bytes 7274496 | tf_op jit(solution)/shard_map/reshape | solution.py:61
  282.9 3.9 fusion.19
  287.5 26.5 %all-gather.7.cloned.1.call-done = f32[3072,128]{0,1:T(8,128)} async-done(((f32[384,128]{0,1:T(8,128)}), f32[3072,128]{0,1:T(8,128)}) %all-gather.7.cloned.1.call-update) | async-done | bytes 1572880 | tf_op jit(solution)/shard_map/all_gather | solution.py:71
  319.7 5.3 %reshape.226 = bf16[32,12,3584]{2,1,0:T(8,128)(2,1)} reshape(bf16[384,3584]{1,0:T(8,128)(2,1)} %fusion.1) | data formatting | bytes 5505024 | tf_op jit(solution)/shard_map/reshape | solution.py:81
  325.0 33.4 %all-to-all-done.2 = bf16[32,12,3584]{2,1,0:T(8,128)(2,1)} async-done(((bf16[32,12,3584]{2,1,0:T(8,128)(2,1)}), bf16[32,12,3584]{2,1,0:T(8,128)(2,1)}, u32[]{:S(2)}, u32[]{:S(2)}) %all-to-all-start.2) | async-done | bytes 2752544 | tf_op jit(solution)/shard_map/all_to_all | solution.py:82
  358.4 5.5 %all-to-all-start.3 = ((bf16[32,12,3584]{2,1,0:T(8,128)(2,1)}), bf16[32,12,3584]{2,1,0:T(8,128)(2,1)}, u32[]{:S(2)}, u32[]{:S(2)}) async-start(bf16[32,12,3584]{2,1,0:T(8,128)(2,1)} %reshape.226), calls=%async_computation.3 | async-start | bytes 7340032 | tf_op jit(solution)/shard_map/all_to_all | solution.py:82
  370.2 3.9 add_convert_fusion
  374.1 75.5 %all-to-all-done.3 = bf16[32,12,3584]{2,1,0:T(8,128)(2,1)} async-done(((bf16[32,12,3584]{2,1,0:T(8,128)(2,1)}), bf16[32,12,3584]{2,1,0:T(8,128)(2,1)}, u32[]{:S(2)}, u32[]{:S(2)}) %all-to-all-start.3) | async-done | bytes 2752544 | tf_op jit(solution)/shard_map/all_to_all | solution.py:82
  449.5 7.0 %pad_maximum_fusion = bf16[32,24,3584]{2,1,0:T(8,128)(2,1)} fusion(bf16[32,12,3584]{2,1,0:T(8,128)(2,1)} %all-to-all-done.3, bf16[32,12,3584]{2,1,0:T(8,128)(2,1)} %all-to-all-done.2), kind=kLoop, calls=%fused_computation.8 | loop fusion | flops 11010048 | bytes 11010048 | tf_op jit(solution)/shard_map/concatenate | solution.py:89
  456.6 8.0 %gather_fusion.2 = bf16[256,3584]{1,0:T(8,128)(2,1)} fusion(bf16[768,3584]{1,0:T(8,128)(2,1)} %bitcast.56, s32[1024]{0:T(1024)S(1)} %pad_clamp_fusion), kind=kCustom, calls=%fused_computation.2 | custom fusion | bytes 3671040 | tf_op jit(solution)/shard_map/gather | solution.py:92
  (59 shorter events, 32.8 us)
Async XLA Ops:
  7.2 156.7 %copy-start = (bf16[8,64,1024]{2,1,0:T(8,128)(2,1)S(1)}, bf16[8,64,1024]{2,1,0:T(8,128)(2,1)}, u32[]{:S(2)}) copy-start(bf16[8,64,1024]{2,1,0:T(8,128)(2,1)} %param.9) | copy-start | bytes 3145732
  27.2 120.8 %all-to-all-start = ((bf16[32,12,4736]{2,1,0:T(8,128)(2,1)}), bf16[32,12,4736]{2,1,0:T(8,128)(2,1)}, u32[]{:S(2)}, u32[]{:S(2)}) async-start(bf16[32,12,4736]{2,1,0:T(8,128)(2,1)} %broadcast_select_fusion.1), calls=%async_computation | async-start | bytes 9699328 | tf_op jit(solution)/shard_map/all_to_all | solution.py:57
  148.0 116.8 %all-to-all-start.1 = ((bf16[32,12,4736]{2,1,0:T(8,128)(2,1)}), bf16[32,12,4736]{2,1,0:T(8,128)(2,1)}, u32[]{:S(2)}, u32[]{:S(2)}) async-start(bf16[32,12,4736]{2,1,0:T(8,128)(2,1)} %broadcast_select_fusion), calls=%async_computation.1 | async-start | bytes 9699328 | tf_op jit(solution)/shard_map/all_to_all | solution.py:57
  155.7 41.1 %all-gather.5.cloned.1.call-start = ((), (), s32[]{:S(2)}) async-start(), calls=%async_computation.4 | async-start | bytes 1769472 | tf_op jit(solution)/shard_map/all_gather | solution.py:71
  162.6 3.1 copy-start.1
  196.8 2.5 copy-start.2
  264.8 93.6 %all-to-all-start.2 = ((bf16[32,12,3584]{2,1,0:T(8,128)(2,1)}), bf16[32,12,3584]{2,1,0:T(8,128)(2,1)}, u32[]{:S(2)}, u32[]{:S(2)}) async-start(bf16[32,12,3584]{2,1,0:T(8,128)(2,1)} %reshape.225), calls=%async_computation.2 | async-start | bytes 7340032 | tf_op jit(solution)/shard_map/all_to_all | solution.py:82
  272.7 41.3 %all-gather.7.cloned.1.call-start = ((), (), s32[]{:S(2)}) async-start(), calls=%async_computation.5 | async-start | bytes 1769472 | tf_op jit(solution)/shard_map/all_gather | solution.py:71
  279.8 3.1 copy-start.3
  313.9 2.5 copy-start.4
  358.4 91.1 %all-to-all-start.3 = ((bf16[32,12,3584]{2,1,0:T(8,128)(2,1)}), bf16[32,12,3584]{2,1,0:T(8,128)(2,1)}, u32[]{:S(2)}, u32[]{:S(2)}) async-start(bf16[32,12,3584]{2,1,0:T(8,128)(2,1)} %reshape.226), calls=%async_computation.3 | async-start | bytes 7340032 | tf_op jit(solution)/shard_map/all_to_all | solution.py:82
  364.0 2.3 copy-start.5
  366.3 2.2 copy-start.6
Sparse Core Ops, SparseCore 0:
  170.5 26.3 all-gather.4
  287.6 26.2 all-gather.6
